TPU v7x, 32 devices: a whole 2x2x4 slice. The times are simulated.
32 devices in a mesh: px: 16 (over z, y, x), py: 2 (over core).
Axes of the slice: x: 2, y: 2, z: 4, core: 2. Of those that a mesh axis runs over, the one named last changes fastest.
Arguments:
- start_value: float32 [128, 256, 256], P(None, 'px', 'py'), may hold values from -6 to 6
- prior: float32 [128, 256, 256], P('px', None, 'py'), may hold values from -6 to 6
- reach: float32 [256, 256], P('px', 'py'), may hold values from -6 to 6
- avoid: float32 [256, 256], P('px', 'py'), may hold values from -3 to 0.5
Outputs:
- final_value: float32 [128, 256, 256], P(None, 'px', 'py')
All inputs are finite; a program needn't handle non-finite values.
Results may differ from a plain program's by a relative error of at most 0.00002.
Values sent between devices are 32-bit elements; how exact they have to be, the bound alone decides.
No kernel may reach another device: no remote copies, remote signals or barrier semaphores. Data moves between devices by JAX's collectives and lax.ppermute only.
A program may use at most 64 MiB of HBM per device.

v0:
```python
import math
import jax
import jax.numpy as jnp
from jax import lax
from jax.sharding import PartitionSpec as P

epsilon = 1e-06
spacing = 1.0 / 64.0
speed = 1.0
turn_rate = 2.0
courant = 0.5


def extended_2(block, sides, width):
    for axis, dim in sides:
        count = lax.axis_size(axis)
        forward = [(i, i + 1) for i in range(count - 1)]
        backward = [(target, source) for source, target in forward]
        low = lax.ppermute(
            lax.slice_in_dim(block, block.shape[dim] - width, None, axis=dim), axis, forward
        )
        high = lax.ppermute(lax.slice_in_dim(block, 0, width, axis=dim), axis, backward)
        block = jnp.concatenate([low, block, high], axis=dim)
    return block


def upwind_blend(first, second, third, fourth, fifth):
    stencil_one = first / 3.0 - 7.0 * second / 6.0 + 11.0 * third / 6.0
    stencil_two = -second / 6.0 + 5.0 * third / 6.0 + fourth / 3.0
    stencil_three = third / 3.0 + 5.0 * fourth / 6.0 - fifth / 6.0
    smooth_one = 13.0 / 12.0 * jnp.square(first - 2.0 * second + third) + 0.25 * jnp.square(
        first - 4.0 * second + 3.0 * third
    )
    smooth_two = 13.0 / 12.0 * jnp.square(second - 2.0 * third + fourth) + 0.25 * jnp.square(
        second - fourth
    )
    smooth_three = 13.0 / 12.0 * jnp.square(third - 2.0 * fourth + fifth) + 0.25 * jnp.square(
        3.0 * third - 4.0 * fourth + fifth
    )
    weight_one = 0.1 / jnp.square(epsilon + smooth_one)
    weight_two = 0.6 / jnp.square(epsilon + smooth_two)
    weight_three = 0.3 / jnp.square(epsilon + smooth_three)
    total = weight_one * stencil_one + weight_two * stencil_two + weight_three * stencil_three
    return total / (weight_one + weight_two + weight_three)


def one_sided(padded, along, length, width):
    slopes = (
        lax.slice_in_dim(padded, 1, length + 6, axis=along)
        - lax.slice_in_dim(padded, 0, length + 5, axis=along)
    ) / width
    pieces = [lax.slice_in_dim(slopes, offset, offset + length, axis=along) for offset in range(6)]
    backward = upwind_blend(pieces[0], pieces[1], pieces[2], pieces[3], pieces[4])
    forward = upwind_blend(pieces[5], pieces[4], pieces[3], pieces[2], pieces[1])
    return (backward, forward)


def change_rate(extended):
    headings = extended.shape[0]
    row_count = extended.shape[1] - 6
    col_count = extended.shape[2] - 6
    heading_gap = 2.0 * math.pi / headings
    center = extended[:, 3 : 3 + row_count, 3 : 3 + col_count]
    west_slope, east_slope = one_sided(extended[:, :, 3 : 3 + col_count], 1, row_count, spacing)
    south_slope, north_slope = one_sided(extended[:, 3 : 3 + row_count, :], 2, col_count, spacing)
    wrapped = jnp.concatenate([center[headings - 3 :], center, center[:3]], axis=0)
    right_slope, left_slope = one_sided(wrapped, 0, headings, heading_gap)
    angles = heading_gap * jnp.arange(headings, dtype=jnp.float32)
    cosine = jnp.cos(angles)[:, None, None]
    sine_value = jnp.sin(angles)[:, None, None]
    result = cosine * speed * 0.5 * (west_slope + east_slope) + sine_value * speed * 0.5 * (
        south_slope + north_slope
    )
    result = result - turn_rate * jnp.abs(0.5 * (right_slope + left_slope))
    result = result + speed * jnp.abs(cosine) * 0.5 * (east_slope - west_slope)
    result = result + speed * jnp.abs(sine_value) * 0.5 * (north_slope - south_slope)
    return result + turn_rate * 0.5 * (left_slope - right_slope)


def section_update(extended):
    headings = extended.shape[0]
    heading_gap = 2.0 * math.pi / headings
    time_step = courant / (2.0 * speed / spacing + turn_rate / heading_gap)
    center = extended[:, 3 : extended.shape[1] - 3, 3 : extended.shape[2] - 3]
    return center + time_step * change_rate(extended)


def trim(field, margin):
    return field[:, margin : field.shape[1] - margin, margin : field.shape[2] - margin]


def on_device(start_value, prior, reach, avoid):
    regrouped = lax.all_to_all(prior, "px", split_axis=1, concat_axis=0, tiled=True)
    tile_rows = start_value.shape[1]
    tile_cols = start_value.shape[2]
    values = start_value
    row_pos = lax.axis_index("px") * tile_rows - 9 + jnp.arange(tile_rows + 18, dtype=jnp.int32)
    col_pos = lax.axis_index("py") * tile_cols - 9 + jnp.arange(tile_cols + 18, dtype=jnp.int32)
    row_inside = (row_pos >= 0) & (row_pos < tile_rows * lax.axis_size("px"))
    col_inside = (col_pos >= 0) & (col_pos < tile_cols * lax.axis_size("py"))
    inside = (row_inside[:, None] & col_inside[None, :]).astype(jnp.float32)[None]
    extended = extended_2(values, (("px", 1), ("py", 2)), 9)
    first = section_update(extended) * trim(inside, 3)
    second = (0.75 * trim(extended, 6) + 0.25 * section_update(first)) * trim(inside, 6)
    third = trim(extended, 9) / 3.0 + 2.0 / 3.0 * section_update(second)
    values = jnp.minimum(regrouped, jnp.maximum(avoid[None], jnp.minimum(reach[None], third)))
    return values


def solution(mesh):
    return jax.shard_map(
        on_device,
        mesh=mesh,
        in_specs=(P(None, "px", "py"), P("px", None, "py"), P("px", "py"), P("px", "py")),
        out_specs=P(None, "px", "py"),
        check_vma=False,
    )
```

profile of v0, /device:TPU:19, one launch (start us, length us, event | category | flops | bytes accessed | tf_op | source)
XLA Modules:
  0.0 142.8 jit_solution(3829122154147356272)
XLA Ops:
  0.0 1.7 %fusion.18 = (f32[128,9,128]{2,1,0:T(8,128)S(1)}, f32[128,9,128]{2,1,0:T(8,128)S(1)}) fusion(f32[128,16,128]{2,1,0:T(8,128)} %param.4), kind=kLoop, calls=%fused_computation.45 | loop fusion | bytes 2359296 | tf_op jit(solution)/shard_map/slice | solution.py:20
  1.9 3.3 %collective-permute-start = (f32[128,9,128]{2,0,1:T(8,128)S(1)}, f32[128,9,128]{2,0,1:T(8,128)}, u32[]{:S(2)}, u32[]{:S(2)}) collective-permute-start(f32[128,9,128]{2,0,1:T(8,128)S(1)} %copy.53), channel_id=1, source_target_pairs={{0,2},{2,4},{4,6},{6,8},{8,10},{10,12},{12,14},{14,16},{16,18},{18... | collective-permute-start | bytes 1769480 | tf_op jit(solution)/shard_map/ppermute | solution.py:19
  5.4 2.3 %collective-permute-start.1 = (f32[128,9,128]{2,0,1:T(8,128)S(1)}, f32[128,9,128]{2,0,1:T(8,128)}, u32[]{:S(2)}, u32[]{:S(2)}) collective-permute-start(f32[128,9,128]{2,0,1:T(8,128)S(1)} %copy.54), channel_id=1, source_target_pairs={{2,0},{4,2},{6,4},{8,6},{10,8},{12,10},{14,12},{16,14},{18,16},{20... | collective-permute-start | bytes 1769480 | tf_op jit(solution)/shard_map/ppermute | solution.py:22
  7.7 1.6 %copy.37 = f32[8,256,128]{2,0,1:T(8,128)} copy(f32[8,256,128]{2,1,0:T(8,128)S(1)} %copy-done.2) | data formatting | bytes 2097152 | tf_op args[1]
  9.3 7.3 %all-to-all-start = ((f32[8,256,128]{2,0,1:T(8,128)}), f32[8,256,128]{2,0,1:T(8,128)}, u32[]{:S(2)}, u32[]{:S(2)}) async-start(f32[8,256,128]{2,0,1:T(8,128)} %copy.37), calls=%async_computation | async-start | bytes 2097152 | tf_op jit(solution)/shard_map/all_to_all | solution.py:93
  16.6 0.4 copy.40
  17.3 16.9 %collective-permute-done = f32[128,9,128]{2,0,1:T(8,128)} collective-permute-done((f32[128,9,128]{2,0,1:T(8,128)S(1)}, f32[128,9,128]{2,0,1:T(8,128)}, u32[]{:S(2)}, u32[]{:S(2)}) %collective-permute-start) | collective-permute-done | bytes 589856 | tf_op jit(solution)/shard_map/ppermute | solution.py:19
  34.3 1.3 copy.43
  35.6 8.1 %collective-permute-done.1 = f32[128,9,128]{2,0,1:T(8,128)} collective-permute-done((f32[128,9,128]{2,0,1:T(8,128)S(1)}, f32[128,9,128]{2,0,1:T(8,128)}, u32[]{:S(2)}, u32[]{:S(2)}) %collective-permute-start.1) | collective-permute-done | bytes 589856 | tf_op jit(solution)/shard_map/ppermute | solution.py:22
  43.7 1.3 copy.45
  45.1 1.3 collective-permute-start.2
  46.4 4.2 %collective-permute-start.3 = (f32[128,34,9]{0,1,2:T(8,128)S(1)}, f32[128,34,9]{0,1,2:T(8,128)S(1)}, u32[]{:S(2)}, u32[]{:S(2)}) collective-permute-start(f32[128,34,9]{0,1,2:T(8,128)S(1)} %copy.47), channel_id=1, source_target_pairs={{1,0},{3,2},{5,4},{7,6},{9,8},{11,10},{13,12},{15,14},{17,16},{19,... | collective-permute-start | bytes 470024 | tf_op jit(solution)/shard_map/ppermute | solution.py:22
  50.8 0.9 collective-permute-done.3
  52.0 0.7 fusion.15
  52.8 0.3 fusion.2
  53.1 0.3 fusion.3
  53.4 1.7 %pad_maximum_fusion = f32[134,28,140]{0,2,1:T(8,128)S(1)} fusion(f32[3,28,140]{0,2,1:T(8,128)S(1)} %get-tuple-element.6, f32[128,28,140]{0,2,1:T(8,128)S(1)} %slice.380, f32[3,28,140]{0,2,1:T(8,128)S(1)} %get-tuple-element.5), kind=kLoop, calls=%fused_computation.2 | loop fusion | flops 1050560 | bytes 4202240 | tf_op jit(solution)/shard_map/concatenate | solution.py:66
  55.1 1.1 fusion
  56.2 29.6 %add_multiply_fusion = f32[128,28,140]{0,2,1:T(8,128)S(1)} fusion(f32[133,28,140]{0,2,1:T(8,128)S(1)} %fusion, f32[128,28,145]{0,2,1:T(8,128)S(1)} %fusion.3, f32[128,33,140]{0,2,1:T(8,128)S(1)} %fusion.2, f32[28,140]{1,0:T(8,128)S(1)} %slice_bitcast_fusion, f32[128]{0:T(128)S(1)} %get-tuple-element.15, f32[128]{0:T(128)S(1)} %get-tuple-element.16, ...), kind=kLoop, calls=%fused_computation.14 | loop fusion | flops 197191680 | bytes 40158528 | tf_op jit(solution)/shard_map/mul | solution.py:103
  85.8 0.5 fusion.16
  86.5 0.3 fusion.5
  86.9 1.3 pad_maximum_fusion.1
  88.2 0.9 fusion.1
  89.1 22.1 %fusion.8 = f32[128,22,134]{0,2,1:T(8,128)S(1)} fusion(f32[128,34,146]{0,2,1:T(8,128)S(1)} %pad_maximum_fusion.2, f32[133,22,134]{0,2,1:T(8,128)S(1)} %fusion.1, f32[128,22,139]{0,2,1:T(8,128)S(1)} %fusion.6, f32[128,27,134]{0,2,1:T(8,128)S(1)} %fusion.5, f32[22,134]{1,0:T(8,128)S(1)} %slice_bitcast_fusion.1, f32[128]{0:T(128)S(1)} %get-tuple-element.15, ...), kind=kLoop, calls=%fused_computation.21 | loop fusion | flops 149428224 | bytes 31710736 | tf_op jit(solution)/shard_map/mul | solution.py:104
  111.3 0.4 fusion.17
  111.7 0.9 pad_maximum_fusion.3
  112.7 1.3 fusion.9
  114.0 2.0 %fusion.4 = f32[133,16,128]{0,2,1:T(8,128)} fusion(f32[134,16,128]{0,2,1:T(8,128)S(1)} %pad_maximum_fusion.3), kind=kLoop, calls=%fused_computation.12 | loop fusion | flops 544768 | bytes 3268608 | tf_op jit(solution)/shard_map/div | solution.py:48
  116.0 2.4 %copy.39 = f32[16,8,16,128]{3,2,1,0:T(8,128)} copy(f32[16,8,16,128]{3,1,2,0:T(8,128)} %bitcast.2) | data formatting | bytes 2097152 | tf_op jit(solution)/shard_map/all_to_all | solution.py:93
  118.4 2.6 %copy.50 = f32[128,16,128]{0,2,1:T(8,128)} copy(f32[128,16,128]{2,1,0:T(8,128)} %bitcast.8) | data formatting | bytes 2097152 | tf_op jit(solution)/shard_map/all_to_all | solution.py:93
  121.0 19.2 %maximum_minimum_fusion = f32[128,16,128]{0,2,1:T(8,128)} fusion(f32[128,16,128]{0,2,1:T(8,128)} %copy.50, f32[133,16,128]{0,2,1:T(8,128)} %fusion.4, f32[128,16,133]{0,2,1:T(8,128)S(1)} %fusion.10, f32[128,21,128]{0,2,1:T(8,128)} %fusion.9, f32[128,16,128]{0,2,1:T(8,128)} %copy-done, f32[128]{0:T(128)S(1)} %get-tuple-element.15, ...), kind=kLoop, calls=%fused_computation.26 | loop fusion | flops 104333312 | bytes 23087104 | tf_op jit(solution)/shard_map/min | solution.py:106
  140.2 2.6 %copy.51 = f32[128,16,128]{2,1,0:T(8,128)} copy(f32[128,16,128]{0,2,1:T(8,128)} %maximum_minimum_fusion) | data formatting | bytes 2097152 | tf_op jit(solution)/shard_map/min | solution.py:106
  (32 shorter events, 1.9 us)
Async XLA Ops:
  1.7 6.0 %copy-start.2 = (f32[8,256,128]{2,1,0:T(8,128)S(1)}, f32[8,256,128]{2,1,0:T(8,128)}, u32[]{:S(2)}) copy-start(f32[8,256,128]{2,1,0:T(8,128)} %param.5) | copy-start | bytes 3145732
  1.9 32.4 %collective-permute-start = (f32[128,9,128]{2,0,1:T(8,128)S(1)}, f32[128,9,128]{2,0,1:T(8,128)}, u32[]{:S(2)}, u32[]{:S(2)}) collective-permute-start(f32[128,9,128]{2,0,1:T(8,128)S(1)} %copy.53), channel_id=1, source_target_pairs={{0,2},{2,4},{4,6},{6,8},{8,10},{10,12},{12,14},{14,16},{16,18},{18... | collective-permute-start | bytes 1769480 | tf_op jit(solution)/shard_map/ppermute | solution.py:19
  5.4 11.2 %copy-start.1 = (f32[128,16,128]{2,1,0:T(8,128)S(1)}, f32[128,16,128]{2,1,0:T(8,128)}, u32[]{:S(2)}) copy-start(f32[128,16,128]{2,1,0:T(8,128)} %param.4) | copy-start | bytes 3145732
  5.4 38.3 %collective-permute-start.1 = (f32[128,9,128]{2,0,1:T(8,128)S(1)}, f32[128,9,128]{2,0,1:T(8,128)}, u32[]{:S(2)}, u32[]{:S(2)}) collective-permute-start(f32[128,9,128]{2,0,1:T(8,128)S(1)} %copy.54), channel_id=1, source_target_pairs={{2,0},{4,2},{6,4},{8,6},{10,8},{12,10},{14,12},{16,14},{18,16},{20... | collective-permute-start | bytes 1769480 | tf_op jit(solution)/shard_map/ppermute | solution.py:22
  9.3 106.7 %all-to-all-start = ((f32[8,256,128]{2,0,1:T(8,128)}), f32[8,256,128]{2,0,1:T(8,128)}, u32[]{:S(2)}, u32[]{:S(2)}) async-start(f32[8,256,128]{2,0,1:T(8,128)} %copy.37), calls=%async_computation | async-start | bytes 2097152 | tf_op jit(solution)/shard_map/all_to_all | solution.py:93
  17.1 34.6 %copy-start = (f32[128,16,128]{0,2,1:T(8,128)}, f32[128,16,128]{0,2,1:T(8,128)S(1)}, u32[]{:S(2)}) copy-start(f32[128,16,128]{0,2,1:T(8,128)S(1)} %copy.40) | copy-start | bytes 3145732
  45.1 5.6 %collective-permute-start.2 = (f32[128,34,9]{0,1,2:T(8,128)S(1)}, f32[128,34,9]{0,1,2:T(8,128)S(1)}, u32[]{:S(2)}, u32[]{:S(2)}) collective-permute-start(f32[128,34,9]{0,1,2:T(8,128)S(1)} %copy.46), channel_id=1, source_target_pairs={{0,1},{2,3},{4,5},{6,7},{8,9},{10,11},{12,13},{14,15},{16,17},{18,... | collective-permute-start | bytes 470024 | tf_op jit(solution)/shard_map/ppermute | solution.py:19
  46.4 5.2 %collective-permute-start.3 = (f32[128,34,9]{0,1,2:T(8,128)S(1)}, f32[128,34,9]{0,1,2:T(8,128)S(1)}, u32[]{:S(2)}, u32[]{:S(2)}) collective-permute-start(f32[128,34,9]{0,1,2:T(8,128)S(1)} %copy.47), channel_id=1, source_target_pairs={{1,0},{3,2},{5,4},{7,6},{9,8},{11,10},{13,12},{15,14},{17,16},{19,... | collective-permute-start | bytes 470024 | tf_op jit(solution)/shard_map/ppermute | solution.py:22
  116.0 5.0 %copy-start.3 = (f32[16,128]{1,0:T(8,128)S(1)}, f32[16,128]{1,0:T(8,128)}, u32[]{:S(2)}) copy-start(f32[16,128]{1,0:T(8,128)} %param.6) | copy-start | bytes 24580
  116.0 5.0 %copy-start.4 = (f32[16,128]{1,0:T(8,128)S(1)}, f32[16,128]{1,0:T(8,128)}, u32[]{:S(2)}) copy-start(f32[16,128]{1,0:T(8,128)} %param.7) | copy-start | bytes 24580
where the time goes:
time: 143 us
  other arithmetic  81.6 us (57%)
  waiting for transfers between devices  25.9 us (18%)
  starting transfers between devices  18.4 us (13%)
  local copies, waits for them, and re-layouts  16.6 us (12%)
    mul x1, other arithmetic, on_device(): first = section_update(extended) * trim(inside, 3)  29.6 us
    mul x1, other arithmetic, on_device(): (0.75 * trim(extended, 6) + 0.25 * section_update(first)) * trim(inside, 6)  22.1 us
    min x1, other arithmetic, on_device(): jnp.minimum(regrouped, jnp.maximum(avoid[None], jnp.minimum(reach[None],...  19.2 us
    ppermute x2, waiting for transfers between devices, extended_2(): lax.ppermute(lax.slice_in_dim(block, block.shape[dim] - width, None, axis...  16.9 us
    ppermute x2, waiting for transfers between devices, extended_2(): lax.ppermute(lax.slice_in_dim(block, 0, width, axis=dim), axis, backward)  8.95 us
    all_to_all x1, starting transfers between devices, on_device(): lax.all_to_all(prior, 'px', split_axis=1, concat_axis=0, tiled=True)  7.34 us
    ppermute x2, starting transfers between devices, extended_2(): lax.ppermute(lax.slice_in_dim(block, 0, width, axis=dim), axis, backward)  6.47 us
    div x9, other arithmetic, one_sided(): (lax.slice_in_dim(padded, 1, length + 6, axis=along) - lax.slice_in_dim(p...  6.45 us
  transfers between devices with their start and end apart: 5, of which 3 were waited for; matrix products, arithmetic and copies ran while one was open for 49% of the time, Pallas kernels for 0%

commit v1 on v0

--- a/solution.py
+++ b/solution.py
@@ -90,7 +90,9 @@
 
 
 def on_device(start_value, prior, reach, avoid):
-    regrouped = lax.all_to_all(prior, "px", split_axis=1, concat_axis=0, tiled=True)
+    regrouped = jnp.concatenate(
+        lax.all_to_all(jnp.stack(jnp.split(prior, lax.axis_size("px"), axis=1)), "px", 0, 0), axis=0
+    )
     tile_rows = start_value.shape[1]
     tile_cols = start_value.shape[2]
     values = start_value

time: 143 us -> 136 us (0.951)
  the two profiles are of different devices: /device:TPU:19 before, /device:TPU:3 now
where the time goes in v1:
time: 136 us
  other arithmetic  81.6 us (60%)
  starting transfers between devices  23 us (17%)
  local copies, waits for them, and re-layouts  22.7 us (17%)
  waiting for transfers between devices  7.89 us (6%)
    mul x1, other arithmetic, on_device(): first = section_update(extended) * trim(inside, 3)  29.6 us
    mul x1, other arithmetic, on_device(): (0.75 * trim(extended, 6) + 0.25 * section_update(first)) * trim(inside, 6)  22.1 us
    min x1, other arithmetic, on_device(): jnp.minimum(regrouped, jnp.maximum(avoid[None], jnp.minimum(reach[None],...  19.2 us
    ppermute x2, starting transfers between devices, extended_2(): lax.ppermute(lax.slice_in_dim(block, 0, width, axis=dim), axis, backward)  11.7 us
    unnamed x28, local copies, waits for them, and re-layouts  10.3 us
    all_to_all x1, starting transfers between devices, on_device(): lax.all_to_all(jnp.stack(jnp.split(prior, lax.axis_size('px'), axis=1)),...  6.75 us
    div x9, other arithmetic, one_sided(): (lax.slice_in_dim(padded, 1, length + 6, axis=along) - lax.slice_in_dim(p...  6.45 us
    ppermute x2, waiting for transfers between devices, extended_2(): lax.ppermute(lax.slice_in_dim(block, block.shape[dim] - width, None, axis...  4.92 us
  transfers between devices with their start and end apart: 5, of which 3 were waited for; matrix products, arithmetic and copies ran while one was open for 58% of the time, Pallas kernels for 0%

profile of v1, /device:TPU:3, one launch (start us, length us, event | category | flops | bytes accessed | tf_op | source)
XLA Modules:
  0.0 135.6 jit_solution(5579672382028182673)
XLA Ops:
  0.0 1.7 %fusion.18 = (f32[128,9,128]{2,1,0:T(8,128)S(1)}, f32[128,9,128]{2,1,0:T(8,128)S(1)}) fusion(f32[128,16,128]{2,1,0:T(8,128)} %param.4), kind=kLoop, calls=%fused_computation.61 | loop fusion | bytes 2359296 | tf_op jit(solution)/shard_map/slice | solution.py:20
  1.9 3.3 %collective-permute-start = (f32[128,9,128]{2,0,1:T(8,128)S(1)}, f32[128,9,128]{2,0,1:T(8,128)}, u32[]{:S(2)}, u32[]{:S(2)}) collective-permute-start(f32[128,9,128]{2,0,1:T(8,128)S(1)} %copy.35), channel_id=1, source_target_pairs={{0,2},{2,4},{4,6},{6,8},{8,10},{10,12},{12,14},{14,16},{16,18},{18... | collective-permute-start | bytes 1769480 | tf_op jit(solution)/shard_map/ppermute | solution.py:19
  5.4 3.0 %collective-permute-start.1 = (f32[128,9,128]{2,0,1:T(8,128)S(1)}, f32[128,9,128]{2,0,1:T(8,128)}, u32[]{:S(2)}, u32[]{:S(2)}) collective-permute-start(f32[128,9,128]{2,0,1:T(8,128)S(1)} %copy.36), channel_id=1, source_target_pairs={{2,0},{4,2},{6,4},{8,6},{10,8},{12,10},{14,12},{16,14},{18,16},{20... | collective-permute-start | bytes 1769480 | tf_op jit(solution)/shard_map/ppermute | solution.py:22
  8.4 0.6 bitcast_dynamic-update-slice_fusion.15
  9.0 0.6 bitcast_dynamic-update-slice_fusion.14
  9.7 0.6 bitcast_dynamic-update-slice_fusion.13
  10.3 0.6 bitcast_dynamic-update-slice_fusion.12
  10.9 0.6 bitcast_dynamic-update-slice_fusion.11
  11.6 0.6 bitcast_dynamic-update-slice_fusion.10
  12.2 0.6 bitcast_dynamic-update-slice_fusion.9
  12.8 0.6 bitcast_dynamic-update-slice_fusion.8
  18.5 6.8 %all-to-all-start = ((f32[16,8,16,128]{3,2,1,0:T(8,128)}), f32[16,8,16,128]{3,2,1,0:T(8,128)}, u32[]{:S(2)}, u32[]{:S(2)}) async-start(f32[16,8,16,128]{3,2,1,0:T(8,128)} %bitcast_dynamic-update-slice_fusion), calls=%async_computation | async-start | bytes 2097152 | tf_op jit(solution)/shard_map/all_to_all | solution.py:94
  26.0 4.9 %collective-permute-done = f32[128,9,128]{2,0,1:T(8,128)} collective-permute-done((f32[128,9,128]{2,0,1:T(8,128)S(1)}, f32[128,9,128]{2,0,1:T(8,128)}, u32[]{:S(2)}, u32[]{:S(2)}) %collective-permute-start) | collective-permute-done | bytes 589856 | tf_op jit(solution)/shard_map/ppermute | solution.py:19
  30.9 1.3 copy.26
  32.2 2.1 %collective-permute-done.1 = f32[128,9,128]{2,0,1:T(8,128)} collective-permute-done((f32[128,9,128]{2,0,1:T(8,128)S(1)}, f32[128,9,128]{2,0,1:T(8,128)}, u32[]{:S(2)}, u32[]{:S(2)}) %collective-permute-start.1) | collective-permute-done | bytes 589856 | tf_op jit(solution)/shard_map/ppermute | solution.py:22
  34.3 1.3 copy.28
  35.7 1.3 collective-permute-start.2
  37.1 8.8 %collective-permute-start.3 = (f32[128,34,9]{0,1,2:T(8,128)S(1)}, f32[128,34,9]{0,1,2:T(8,128)S(1)}, u32[]{:S(2)}, u32[]{:S(2)}) collective-permute-start(f32[128,34,9]{0,1,2:T(8,128)S(1)} %copy.30), channel_id=1, source_target_pairs={{1,0},{3,2},{5,4},{7,6},{9,8},{11,10},{13,12},{15,14},{17,16},{19,... | collective-permute-start | bytes 470024 | tf_op jit(solution)/shard_map/ppermute | solution.py:22
  46.0 0.9 collective-permute-done.3
  47.2 0.7 fusion.15
  48.6 1.7 %pad_maximum_fusion = f32[134,28,140]{0,2,1:T(8,128)S(1)} fusion(f32[3,28,140]{0,2,1:T(8,128)S(1)} %get-tuple-element.6, f32[128,28,140]{0,2,1:T(8,128)S(1)} %slice.380, f32[3,28,140]{0,2,1:T(8,128)S(1)} %get-tuple-element.5), kind=kLoop, calls=%fused_computation.2 | loop fusion | flops 1050560 | bytes 4202240 | tf_op jit(solution)/shard_map/concatenate | solution.py:66
  50.3 1.1 fusion
  51.4 29.6 %add_multiply_fusion = f32[128,28,140]{0,2,1:T(8,128)S(1)} fusion(f32[133,28,140]{0,2,1:T(8,128)S(1)} %fusion, f32[128,28,145]{0,2,1:T(8,128)S(1)} %fusion.3, f32[128,33,140]{0,2,1:T(8,128)S(1)} %fusion.2, f32[28,140]{1,0:T(8,128)S(1)} %slice_bitcast_fusion, f32[128]{0:T(128)S(1)} %get-tuple-element.15, f32[128]{0:T(128)S(1)} %get-tuple-element.16, ...), kind=kLoop, calls=%fused_computation.14 | loop fusion | flops 197191680 | bytes 40158528 | tf_op jit(solution)/shard_map/mul | solution.py:105
  82.2 1.3 pad_maximum_fusion.1
  83.4 0.9 fusion.1
  84.3 22.1 %fusion.8 = f32[128,22,134]{0,2,1:T(8,128)S(1)} fusion(f32[128,34,146]{0,2,1:T(8,128)S(1)} %pad_maximum_fusion.2, f32[133,22,134]{0,2,1:T(8,128)S(1)} %fusion.1, f32[128,22,139]{0,2,1:T(8,128)S(1)} %fusion.6, f32[128,27,134]{0,2,1:T(8,128)S(1)} %fusion.5, f32[22,134]{1,0:T(8,128)S(1)} %slice_bitcast_fusion.1, f32[128]{0:T(128)S(1)} %get-tuple-element.15, ...), kind=kLoop, calls=%fused_computation.21 | loop fusion | flops 149428224 | bytes 31710736 | tf_op jit(solution)/shard_map/mul | solution.py:106
  106.9 0.9 pad_maximum_fusion.3
  108.0 1.3 fusion.9
  109.3 2.0 %fusion.4 = f32[133,16,128]{0,2,1:T(8,128)} fusion(f32[134,16,128]{0,2,1:T(8,128)S(1)} %pad_maximum_fusion.3), kind=kLoop, calls=%fused_computation.12 | loop fusion | flops 544768 | bytes 3268608 | tf_op jit(solution)/shard_map/div | solution.py:48
  111.2 2.6 %copy.33 = f32[128,16,128]{0,2,1:T(8,128)} copy(f32[128,16,128]{2,1,0:T(8,128)} %bitcast.16) | data formatting | bytes 2097152 | tf_op jit(solution)/shard_map/reshape | solution.py:93
  113.8 19.2 %maximum_minimum_fusion = f32[128,16,128]{0,2,1:T(8,128)} fusion(f32[128,16,128]{0,2,1:T(8,128)} %copy.33, f32[133,16,128]{0,2,1:T(8,128)} %fusion.4, f32[128,16,133]{0,2,1:T(8,128)S(1)} %fusion.10, f32[128,21,128]{0,2,1:T(8,128)} %fusion.9, f32[128,16,128]{0,2,1:T(8,128)} %copy-done, f32[128]{0:T(128)S(1)} %get-tuple-element.15, ...), kind=kLoop, calls=%fused_computation.26 | loop fusion | flops 104333312 | bytes 23087104 | tf_op jit(solution)/shard_map/min | solution.py:108
  133.0 2.6 %copy.34 = f32[128,16,128]{2,1,0:T(8,128)} copy(f32[128,16,128]{0,2,1:T(8,128)} %maximum_minimum_fusion) | data formatting | bytes 2097152 | tf_op jit(solution)/shard_map/min | solution.py:108
  (46 shorter events, 9.2 us)
Async XLA Ops:
  1.7 6.7 %copy-start.2 = (f32[8,256,128]{2,1,0:T(8,128)S(1)}, f32[8,256,128]{2,1,0:T(8,128)}, u32[]{:S(2)}) copy-start(f32[8,256,128]{2,1,0:T(8,128)} %param.5) | copy-start | bytes 3145732
  1.9 29.0 %collective-permute-start = (f32[128,9,128]{2,0,1:T(8,128)S(1)}, f32[128,9,128]{2,0,1:T(8,128)}, u32[]{:S(2)}, u32[]{:S(2)}) collective-permute-start(f32[128,9,128]{2,0,1:T(8,128)S(1)} %copy.35), channel_id=1, source_target_pairs={{0,2},{2,4},{4,6},{6,8},{8,10},{10,12},{12,14},{14,16},{16,18},{18... | collective-permute-start | bytes 1769480 | tf_op jit(solution)/shard_map/ppermute | solution.py:19
  5.4 28.9 %collective-permute-start.1 = (f32[128,9,128]{2,0,1:T(8,128)S(1)}, f32[128,9,128]{2,0,1:T(8,128)}, u32[]{:S(2)}, u32[]{:S(2)}) collective-permute-start(f32[128,9,128]{2,0,1:T(8,128)S(1)} %copy.36), channel_id=1, source_target_pairs={{2,0},{4,2},{6,4},{8,6},{10,8},{12,10},{14,12},{16,14},{18,16},{20... | collective-permute-start | bytes 1769480 | tf_op jit(solution)/shard_map/ppermute | solution.py:22
  9.0 16.3 %copy-start.1 = (f32[128,16,128]{2,1,0:T(8,128)S(1)}, f32[128,16,128]{2,1,0:T(8,128)}, u32[]{:S(2)}) copy-start(f32[128,16,128]{2,1,0:T(8,128)} %param.4) | copy-start | bytes 3145732
  18.5 92.7 %all-to-all-start = ((f32[16,8,16,128]{3,2,1,0:T(8,128)}), f32[16,8,16,128]{3,2,1,0:T(8,128)}, u32[]{:S(2)}, u32[]{:S(2)}) async-start(f32[16,8,16,128]{3,2,1,0:T(8,128)} %bitcast_dynamic-update-slice_fusion), calls=%async_computation | async-start | bytes 2097152 | tf_op jit(solution)/shard_map/all_to_all | solution.py:94
  25.7 21.2 %copy-start = (f32[128,16,128]{0,2,1:T(8,128)}, f32[128,16,128]{0,2,1:T(8,128)S(1)}, u32[]{:S(2)}) copy-start(f32[128,16,128]{0,2,1:T(8,128)S(1)} %copy.23) | copy-start | bytes 3145732
  35.7 10.2 %collective-permute-start.2 = (f32[128,34,9]{0,1,2:T(8,128)S(1)}, f32[128,34,9]{0,1,2:T(8,128)S(1)}, u32[]{:S(2)}, u32[]{:S(2)}) collective-permute-start(f32[128,34,9]{0,1,2:T(8,128)S(1)} %copy.29), channel_id=1, source_target_pairs={{0,1},{2,3},{4,5},{6,7},{8,9},{10,11},{12,13},{14,15},{16,17},{18,... | collective-permute-start | bytes 470024 | tf_op jit(solution)/shard_map/ppermute | solution.py:19
  37.1 9.8 %collective-permute-start.3 = (f32[128,34,9]{0,1,2:T(8,128)S(1)}, f32[128,34,9]{0,1,2:T(8,128)S(1)}, u32[]{:S(2)}, u32[]{:S(2)}) collective-permute-start(f32[128,34,9]{0,1,2:T(8,128)S(1)} %copy.30), channel_id=1, source_target_pairs={{1,0},{3,2},{5,4},{7,6},{9,8},{11,10},{13,12},{15,14},{17,16},{19,... | collective-permute-start | bytes 470024 | tf_op jit(solution)/shard_map/ppermute | solution.py:22
  111.2 2.6 %copy-start.3 = (f32[16,128]{1,0:T(8,128)S(1)}, f32[16,128]{1,0:T(8,128)}, u32[]{:S(2)}) copy-start(f32[16,128]{1,0:T(8,128)} %param.6) | copy-start | bytes 24580
  111.2 2.6 %copy-start.4 = (f32[16,128]{1,0:T(8,128)S(1)}, f32[16,128]{1,0:T(8,128)}, u32[]{:S(2)}) copy-start(f32[16,128]{1,0:T(8,128)} %param.7) | copy-start | bytes 24580
